TPU v7x, 256 devices: a whole 4x4x8 slice. The times are simulated.
256 devices in a mesh: cam: 8 (over x, core), clip: 32 (over y, z).
Axes of the slice: x: 4, y: 4, z: 8, core: 2. Of those that a mesh axis runs over, the one named last changes fastest.
Arguments:
- tokens: bfloat16 [64, 8, 256, 1024], P('clip', 'cam'), may hold values from -6 to 6
- w_query: bfloat16 [1024, 1024], replicated, may hold values from -0.1875 to 0.1875
- w_key: bfloat16 [1024, 1024], replicated, may hold values from -0.1875 to 0.1875
- w_value: bfloat16 [1024, 1024], replicated, may hold values from -0.1875 to 0.1875
- w_proj: bfloat16 [1024, 256], replicated, may hold values from -0.1875 to 0.1875
- prototypes: bfloat16 [256, 65536], P(None, ('cam', 'clip')), may hold values from -6 to 6
Outputs:
- codes: float32 [64, 65536], P(None, ('cam', 'clip'))
- prototype_gradient: float32 [256, 65536], P(None, ('cam', 'clip'))
- grad_proj: float32 [1024, 256], P('clip')
- grad_value: float32 [1024, 1024], P('clip', 'cam')
All inputs are finite; a program needn't handle non-finite values.
Results may differ from a plain program's by a relative error of at most 0.015.
Values may be sent and summed in bfloat16 or wider, within the bound.
A program may use at most 128 MiB of HBM per device.

v0:
```python
import jax
import jax.numpy as jnp
from jax import lax
from jax.sharding import PartitionSpec as P

D = 1024
HD = 64
PROTOS = 65536
TOK = 256
ITERS = 3
H = 16
SINK_EPS = 0.05
SOFTMAX_TEMP = 0.1
NORM_EPS = 1e-06
heads_per_group = 4


def column_sums(query_rows, key_rows, total):
    scores = jnp.einsum(
        "ihe,jhe->hij", query_rows, key_rows, preferred_element_type=jnp.float32
    ) * HD ** (-0.5)
    exponent_values = jnp.exp(scores)
    probs = exponent_values / jnp.sum(exponent_values, axis=2, keepdims=True)
    return jnp.sum(probs, axis=1) / total


def camera_block(query_clip, key_clip, total):
    tokens_here = query_clip.shape[0]
    width = heads_per_group * HD
    parts = []
    for group in range(H // heads_per_group):
        query_group = query_clip[:, group * width : (group + 1) * width].reshape(
            tokens_here, heads_per_group, HD
        )
        key_group = key_clip[:, group * width : (group + 1) * width].reshape(
            total, heads_per_group, HD
        )
        parts.append(column_sums(query_group, key_group, total))
    return jnp.concatenate(parts, axis=0)


def local(tokens, w_query, w_key, w_value, w_proj, prototypes):
    clips = tokens.shape[0]
    own = tokens.reshape(clips, TOK, D)
    query_vectors = jnp.einsum(
        "ctd,de->cte", own, w_query, preferred_element_type=jnp.float32
    ).astype(jnp.bfloat16)
    key_rows = jnp.einsum("ctd,de->cte", own, w_key, preferred_element_type=jnp.float32).astype(
        jnp.bfloat16
    )
    collected_rows = lax.all_gather(key_rows.reshape(clips, 1, TOK, D), "cam", axis=1, tiled=True)
    cameras = collected_rows.shape[1]
    total = cameras * TOK

    def per_clip(clip_pair):
        return camera_block(clip_pair[0], clip_pair[1], total)

    partial_sums = lax.map(per_clip, (query_vectors, collected_rows.reshape(clips, total, D)))
    weights = lax.psum_scatter(
        partial_sums.reshape(clips, H, cameras, TOK), "cam", scatter_dimension=2, tiled=True
    )
    weights = weights.reshape(clips, H, TOK).astype(jnp.bfloat16)
    mixture = jnp.einsum("chj,cjd->chd", weights, own, preferred_element_type=jnp.float32).astype(
        jnp.bfloat16
    )
    head_out = jnp.einsum(
        "chd,dhe->che", mixture, w_value.reshape(D, H, HD), preferred_element_type=jnp.float32
    )
    pooled = lax.psum(head_out.reshape(clips, D), "cam").astype(jnp.bfloat16)
    share_rows = D // lax.axis_size("clip")
    embed = jnp.dot(pooled, w_proj, preferred_element_type=jnp.float32)
    embed_norm = jnp.sqrt(jnp.sum(embed * embed, axis=1, keepdims=True) + NORM_EPS)
    unit = embed / embed_norm
    unit_b = unit.astype(jnp.bfloat16)
    all_units = lax.all_gather(unit_b, "clip", axis=0, tiled=True)
    proto_f = prototypes.astype(jnp.float32)
    column_norm = jnp.sqrt(jnp.sum(proto_f * proto_f, axis=0, keepdims=True) + NORM_EPS)
    unit_proto = proto_f / column_norm
    proto_b = unit_proto.astype(jnp.bfloat16)
    logit_scores = jnp.dot(all_units, proto_b, preferred_element_type=jnp.float32)
    exponent_values = jnp.exp(logit_scores / SOFTMAX_TEMP)
    assign = jnp.exp(logit_scores / SINK_EPS)
    prob_total = lax.psum(jnp.sum(exponent_values, axis=1), ("cam", "clip"))
    first_step = 0
    for step in range(first_step, ITERS):
        assign = assign / jnp.sum(assign, axis=0, keepdims=True)
        row_total = lax.psum(jnp.sum(assign, axis=1), ("cam", "clip"))
        assign = assign / row_total[:, None]
    prob = exponent_values / prob_total[:, None]
    grad_logits = (PROTOS * (prob - assign)).astype(jnp.bfloat16)
    codes = PROTOS * assign
    grad_unit = lax.psum_scatter(
        jnp.dot(grad_logits, proto_b.T, preferred_element_type=jnp.float32),
        "clip",
        scatter_dimension=0,
        tiled=True,
    )
    grad_unit = lax.psum(grad_unit, "cam")
    grad_embed = (grad_unit - unit * jnp.sum(unit * grad_unit, axis=1, keepdims=True)) / embed_norm
    grad_embed_b = grad_embed.astype(jnp.bfloat16)
    grad_pooled = jnp.dot(grad_embed_b, w_proj.T, preferred_element_type=jnp.float32).astype(
        jnp.bfloat16
    )
    piece = pooled
    grad_proj = lax.psum_scatter(
        jnp.einsum("cd,ce->de", piece, grad_embed_b, preferred_element_type=jnp.float32),
        "clip",
        scatter_dimension=0,
        tiled=True,
    )
    grad_heads = grad_pooled.reshape(clips, H, HD)
    piece = lax.slice_in_dim(mixture, 0, share_rows * lax.axis_size("clip"), axis=2)
    value_rows = lax.psum_scatter(
        jnp.einsum("chd,che->dhe", piece, grad_heads, preferred_element_type=jnp.float32).reshape(
            share_rows * lax.axis_size("clip"), D
        ),
        "clip",
        scatter_dimension=0,
        tiled=True,
    )
    grad_value = lax.psum_scatter(value_rows, "cam", scatter_dimension=1, tiled=True)
    grad_unit_proto = jnp.einsum(
        "be,bk->ek", all_units, grad_logits, preferred_element_type=jnp.float32
    )
    prototype_gradient = (
        grad_unit_proto - unit_proto * jnp.sum(unit_proto * grad_unit_proto, axis=0, keepdims=True)
    ) / column_norm
    return (codes, prototype_gradient, grad_proj, grad_value)


def solution(mesh):
    in_specs = (P("clip", "cam", None, None), P(), P(), P(), P(), P(None, ("cam", "clip")))
    out_specs = (
        P(None, ("cam", "clip")),
        P(None, ("cam", "clip")),
        P("clip", None),
        P("clip", "cam"),
    )
    return jax.shard_map(local, mesh=mesh, in_specs=in_specs, out_specs=out_specs, check_vma=False)
```

profile of v0, /device:TPU:8, one launch (start us, length us, event | category | flops | bytes accessed | tf_op | source)
XLA Modules:
  0.0 1159.4 jit_solution(2229369669846176685)
XLA Ops:
  7.2 1.5 copy-done
  8.8 3.5 fusion.32
  12.4 4.0 copy.30
  16.4 3.8 fusion.29
  20.2 47.3 %all-gather.4.cloned.1.call-done = bf16[2,2048,1024]{2,1,0:T(8,128)(2,1)} async-done(((bf16[2,256,1024]{2,1,0:T(8,128)(2,1)}), bf16[2,2048,1024]{2,1,0:T(8,128)(2,1)}) %all-gather.4.cloned.1.call-update) | async-done | bytes 8388624 | tf_op jit(solution)/shard_map/all_gather | solution.py:51
  67.5 130.2 %while.10 = (s32[]{:T(128)}, f32[2,16,2048]{2,1,0:T(8,128)}, bf16[2,256,1024]{2,1,0:T(8,128)(2,1)}, bf16[2,2048,1024]{2,1,0:T(8,128)(2,1)}, s32[]{:T(128)}) while((s32[]{:T(128)}, f32[2,16,2048]{2,1,0:T(8,128)}, bf16[2,256,1024]{2,1,0:T(8,128)(2,1)}, bf16[2,2048,1024]{2,1,0:T(8,128)(2,1)}, s32[]{:T(128)}) %tuple.47), condition=%wide.region_9.10_spmd, body=%wide.region_0.9_spmd.sunk | while | flops 2181148672 | bytes 112328888 | solution.py:58
  67.5 4.6 constant_dynamic-slice_fusion.6
  72.1 6.5 copy.50
  78.6 3.8 fusion.140
  83.2 2.1 copy.49
  87.1 5.7 fusion.143
  92.9 7.5 divide_reduce_fusion.11
  100.3 4.5 fusion.144
  104.8 6.1 divide_reduce_fusion.12
  111.8 4.5 fusion.142
  116.3 5.5 divide_reduce_fusion.10
  121.8 4.5 fusion.141
  126.3 5.6 divide_reduce_fusion.9
  132.7 4.6 constant_dynamic-slice_fusion.6
  137.3 6.5 copy.50
  143.7 3.8 fusion.140
  148.4 2.1 copy.49
  152.3 5.7 fusion.143
  158.0 7.5 divide_reduce_fusion.11
  165.5 4.5 fusion.144
  169.9 6.1 divide_reduce_fusion.12
  176.9 4.5 fusion.142
  181.4 5.5 divide_reduce_fusion.10
  186.9 4.5 fusion.141
  191.4 5.6 divide_reduce_fusion.9
  197.8 1.7 copy.46
  201.4 31.9 %reduce-scatter.5.cloned.1.call-done = f32[2,16,1,256]{3,1,0,2:T(8,128)} async-done(((f32[2,16,8,256]{3,1,0,2:T(8,128)}), f32[2,16,1,256]{3,1,0,2:T(8,128)}) %reduce-scatter.5.cloned.1.call-update) | async-done | bytes 32784 | tf_op jit(solution)/shard_map/reduce_scatter | solution.py:59
  233.3 1.5 convolution_convert_fusion
  234.8 2.2 convolution_bitcast_fusion
  237.1 13.2 %psum.42 = bf16[2,1024]{1,0:T(2,128)(2,1)S(1)} all-reduce(f32[2,1024]{1,0:T(2,128)S(1)} %reshape.88), channel_id=1, replica_groups=mesh['cam'=8,'clip'=32] {'cam'}, use_global_device_ids=true, to_apply=%region_11.12 | all-reduce | flops 2048 | bytes 12288 | tf_op jit(solution)/shard_map/psum | solution.py:69
  250.3 1.3 multiply_reduce_fusion.2
  251.7 43.0 %all-gather.1 = bf16[32,2,256]{2,1,0:T(2,128)(2,1)S(1)} all-gather(bf16[1,2,256]{2,1,0:T(2,128)(2,1)S(1)} %get-tuple-element.51), channel_id=1, replica_groups=mesh['cam'=8,'clip'=32] {'clip'}, dimensions={0}, use_global_device_ids=true | all-gather | bytes 33792 | tf_op jit(solution)/shard_map/all_gather | solution.py:75
  295.1 72.7 %psum.43 = f32[64]{0:T(128)S(1)} all-reduce(f32[64]{0:T(128)S(1)} %get-tuple-element.40), channel_id=1, replica_groups=mesh['cam'=8,'clip'=32] {'cam','clip'}, use_global_device_ids=true, to_apply=%region_16.17 | all-reduce | flops 64 | bytes 512 | tf_op jit(solution)/shard_map/psum | solution.py:87
  368.0 74.3 %psum.44 = f32[64]{0:T(128)S(1)} all-reduce(f32[64]{0:T(128)S(1)} %fusion.48), channel_id=1, replica_groups=mesh['cam'=8,'clip'=32] {'cam','clip'}, use_global_device_ids=true, to_apply=%region_19.20 | all-reduce | flops 64 | bytes 512 | tf_op jit(solution)/shard_map/psum | solution.py:87
  442.6 73.4 %all-reduce.1 = (f32[64]{0:T(128)S(1)}, f32[64]{0:T(128)S(1)}) all-reduce(f32[64]{0:T(128)S(1)} %fusion.50, f32[64]{0:T(128)S(1)} %get-tuple-element.39), channel_id=1, replica_groups=mesh['cam'=8,'clip'=32] {'cam','clip'}, use_global_device_ids=true, to_apply=%region_22.23 | all-reduce | flops 128 | bytes 1024 | tf_op jit(solution)/shard_map/psum | solution.py:87
  518.8 137.5 %all-reduce.4.cloned.1.call-done = f32[64,256]{1,0:T(8,128)} async-done(((f32[64,256]{1,0:T(8,128)}), f32[64,256]{1,0:T(8,128)}) %all-reduce.4.cloned.1.call-update) | async-done | bytes 65552
  657.1 12.4 %psum.47 = f32[2,256]{1,0:T(2,128)S(1)} all-reduce(f32[2,256]{1,0:T(2,128)S(1)} %constant_dynamic-slice_fusion.2), channel_id=1, replica_groups=mesh['cam'=8,'clip'=32] {'cam'}, use_global_device_ids=true, to_apply=%region_27.28 | all-reduce | flops 512 | bytes 4096 | tf_op jit(solution)/shard_map/psum | solution.py:98
  671.0 2.7 fusion.52
  673.7 5.4 copy.35
  679.2 1.3 fusion.59
  680.6 217.1 %reduce-scatter.9.cloned.1.call-done = f32[32,1024]{1,0:T(8,128)} async-done(((f32[1024,1024]{1,0:T(8,128)}), f32[32,1024]{1,0:T(8,128)}) %reduce-scatter.9.cloned.1.call-update) | async-done | bytes 131088 | tf_op jit(solution)/shard_map/reduce_scatter | solution.py:113
  898.7 218.6 %reduce-scatter.7.cloned.1.call-done = f32[32,256]{1,0:T(8,128)} async-done(((f32[1024,256]{1,0:T(8,128)}), f32[32,256]{1,0:T(8,128)}) %reduce-scatter.7.cloned.1.call-update) | async-done | bytes 32784 | tf_op jit(solution)/shard_map/reduce_scatter | solution.py:105
  1117.3 35.2 %reduce-scatter.11.cloned.1.call-done = f32[32,128]{1,0:T(8,128)} async-done(((f32[32,1024]{1,0:T(8,128)}), f32[32,128]{1,0:T(8,128)}) %reduce-scatter.11.cloned.1.call-update) | async-done | bytes 16400 | tf_op jit(solution)/shard_map/reduce_scatter | solution.py:121
  (71 shorter events, 17.1 us)
Async XLA Ops:
  7.2 1.6 copy-start
  7.2 9.2 copy-start.5
  7.2 60.4 %all-gather.4.cloned.1.call-start = ((), (), s32[]{:S(2)}) async-start(), calls=%async_computation.8 | async-start | bytes 9437184 | tf_op jit(solution)/shard_map/all_gather | solution.py:51
  12.3 221.0 %reduce-scatter.5.cloned.1.call-start = ((), (), s32[]{:S(2)}) async-start(), calls=%async_computation.4 | async-start | bytes 294912 | tf_op jit(solution)/shard_map/reduce_scatter | solution.py:59
  67.5 450.1 %copy-start.8 = (u32[256]{0:T(256)S(1)}, u32[256]{0:T(256)}, u32[]{:S(2)}) copy-start(u32[256]{0:T(256)} %constant.40) | copy-start | bytes 3076
  78.6 3.8 copy-start.3
  86.5 0.6 copy-start.2
  126.3 5.6 copy-start.6
  132.0 0.7 copy-start.7
  143.7 3.8 copy-start.3
  151.6 0.6 copy-start.2
  191.4 5.6 copy-start.6
  197.1 0.7 copy-start.7
  199.5 456.9 %all-reduce.4.cloned.1.call-start = ((), (), s32[]{:S(2)}) async-start(), calls=%async_computation.9 | async-start | bytes 131072
  517.5 380.1 %reduce-scatter.9.cloned.1.call-start = ((), (), s32[]{:S(2)}) async-start(), calls=%async_computation.6 | async-start | bytes 4325376 | tf_op jit(solution)/shard_map/reduce_scatter | solution.py:113
  671.0 481.5 %copy-start.1 = (bf16[1024,1024]{1,0:T(8,128)(2,1)S(1)}, bf16[1024,1024]{1,0:T(8,128)(2,1)}, u32[]{:S(2)}) copy-start(bf16[1024,1024]{1,0:T(8,128)(2,1)} %param.10) | copy-start | bytes 6291460
  673.7 224.0 %copy-start.4 = (bf16[256,256]{1,0:T(8,128)(2,1)S(1)}, bf16[256,256]{1,0:T(8,128)(2,1)}, u32[]{:S(2)}) copy-start(bf16[256,256]{1,0:T(8,128)(2,1)} %param.13) | copy-start | bytes 393220
  679.1 438.2 %reduce-scatter.7.cloned.1.call-start = ((), (), s32[]{:S(2)}) async-start(), calls=%async_computation.5 | async-start | bytes 1081344 | tf_op jit(solution)/shard_map/reduce_scatter | solution.py:105
  680.5 472.0 %reduce-scatter.11.cloned.1.call-start = ((), (), s32[]{:S(2)}) async-start(), calls=%async_computation.7 | async-start | bytes 147456 | tf_op jit(solution)/shard_map/reduce_scatter | solution.py:121
Sparse Core Ops, SparseCore 0:
  12.5 55.0 all-gather.3
  199.6 33.6 reduce-scatter.4
  517.7 138.6 all-reduce.3
  679.3 218.3 reduce-scatter.8
  901.9 215.3 reduce-scatter.6
  1120.2 32.2 reduce-scatter.10
where the time goes:
time: 1160 us
  waiting for transfers between devices  688 us (59%)
  blocking collectives  289 us (25%)
  matrix products  107 us (9%)
  local copies, waits for them, and re-layouts  54.6 us (5%)
  between operations  14.9 us (1%)
    psum x3, blocking collectives, local(): row_total = lax.psum(jnp.sum(assign, axis=1), ('cam', 'clip'))  220 us
    reduce_scatter x1, waiting for transfers between devices, local(): lax.psum_scatter(jnp.einsum('cd,ce->de', piece, grad_embed_b, preferred_e...  219 us
    reduce_scatter x1, waiting for transfers between devices, local(): lax.psum_scatter(jnp.einsum('chd,che->dhe', piece, grad_heads, preferred_...  217 us
    unnamed x7, waiting for transfers between devices  138 us
    div x8, matrix products, column_sums(): probs = exponent_values / jnp.sum(exponent_values, axis=2, keepdims=True)  49.5 us
    all_gather x1, waiting for transfers between devices, local(): lax.all_gather(key_rows.reshape(clips, 1, TOK, D), 'cam', axis=1, tiled=T...  47.3 us
    all_gather x1, blocking collectives, local(): all_units = lax.all_gather(unit_b, 'clip', axis=0, tiled=True)  43 us
    dot_general x8, matrix products, column_sums(): jnp.einsum('ihe,jhe->hij', query_rows, key_rows, preferred_element_type=j...  38.4 us
  transfers between devices with their start and end apart: 6, of which 6 were waited for; matrix products, arithmetic and copies ran while one was open for 1% of the time, Pallas kernels for 0%

commit v1 on v0

--- a/solution.py
+++ b/solution.py
@@ -84,7 +84,8 @@
     first_step = 0
     for step in range(first_step, ITERS):
         assign = assign / jnp.sum(assign, axis=0, keepdims=True)
-        row_total = lax.psum(jnp.sum(assign, axis=1), ("cam", "clip"))
+        one_axis = lax.psum(jnp.sum(assign, axis=1), "cam")
+        row_total = lax.psum(one_axis, "clip")
         assign = assign / row_total[:, None]
     prob = exponent_values / prob_total[:, None]
     grad_logits = (PROTOS * (prob - assign)).astype(jnp.bfloat16)

time: 1160 us -> 1260 us (1.086)
  blocking collectives: 289 us -> 391 us
    psum x3 -> x7, blocking collectives: 220 us -> 323 us  [the longest x3 202 us: local(): row_total = lax.psum(one_axis, 'clip')]
where the time goes in v1:
time: 1260 us
  waiting for transfers between devices  686 us (54%)
  blocking collectives  391 us (31%)
  matrix products  107 us (8%)
  local copies, waits for them, and re-layouts  54.6 us (4%)
  between operations  14.9 us (1%)
    reduce_scatter x1, waiting for transfers between devices, local(): lax.psum_scatter(jnp.einsum('cd,ce->de', piece, grad_embed_b, preferred_e...  218 us
    reduce_scatter x1, waiting for transfers between devices, local(): lax.psum_scatter(jnp.einsum('chd,che->dhe', piece, grad_heads, preferred_...  217 us
    psum x3, blocking collectives, local(): row_total = lax.psum(one_axis, 'clip')  202 us
    unnamed x7, waiting for transfers between devices  136 us
    psum x1, blocking collectives, local(): prob_total = lax.psum(jnp.sum(exponent_values, axis=1), ('cam', 'clip'))  83.2 us
    div x8, matrix products, column_sums(): probs = exponent_values / jnp.sum(exponent_values, axis=2, keepdims=True)  49.5 us
    all_gather x1, waiting for transfers between devices, local(): lax.all_gather(key_rows.reshape(clips, 1, TOK, D), 'cam', axis=1, tiled=T...  47.3 us
    all_gather x1, blocking collectives, local(): all_units = lax.all_gather(unit_b, 'clip', axis=0, tiled=True)  43 us
  transfers between devices with their start and end apart: 6, of which 6 were waited for; matrix products, arithmetic and copies ran while one was open for 1% of the time, Pallas kernels for 0%

profile of v1, /device:TPU:8, one launch (start us, length us, event | category | flops | bytes accessed | tf_op | source)
XLA Modules:
  0.0 1259.8 jit_solution(10495705892645997520)
XLA Ops:
  8.8 3.5 fusion.32
  12.4 4.0 copy.30
  16.4 3.8 fusion.29
  20.2 47.3 %all-gather.4.cloned.1.call-done = bf16[2,2048,1024]{2,1,0:T(8,128)(2,1)} async-done(((bf16[2,256,1024]{2,1,0:T(8,128)(2,1)}), bf16[2,2048,1024]{2,1,0:T(8,128)(2,1)}) %all-gather.4.cloned.1.call-update) | async-done | bytes 8388624 | tf_op jit(solution)/shard_map/all_gather | solution.py:51
  67.5 130.2 %while.10 = (s32[]{:T(128)}, f32[2,16,2048]{2,1,0:T(8,128)}, bf16[2,256,1024]{2,1,0:T(8,128)(2,1)}, bf16[2,2048,1024]{2,1,0:T(8,128)(2,1)}, s32[]{:T(128)}) while((s32[]{:T(128)}, f32[2,16,2048]{2,1,0:T(8,128)}, bf16[2,256,1024]{2,1,0:T(8,128)(2,1)}, bf16[2,2048,1024]{2,1,0:T(8,128)(2,1)}, s32[]{:T(128)}) %tuple.47), condition=%wide.region_9.10_spmd, body=%wide.region_0.9_spmd.sunk | while | flops 2181148672 | bytes 112328888 | solution.py:58
  67.5 4.6 constant_dynamic-slice_fusion.6
  72.1 6.5 copy.50
  78.6 3.8 fusion.140
  83.2 2.1 copy.49
  87.1 5.7 fusion.143
  92.9 7.5 divide_reduce_fusion.11
  100.3 4.5 fusion.144
  104.8 6.1 divide_reduce_fusion.12
  111.8 4.5 fusion.142
  116.3 5.5 divide_reduce_fusion.10
  121.8 4.5 fusion.141
  126.3 5.6 divide_reduce_fusion.9
  132.7 4.6 constant_dynamic-slice_fusion.6
  137.3 6.5 copy.50
  143.7 3.8 fusion.140
  148.4 2.1 copy.49
  152.3 5.7 fusion.143
  158.0 7.5 divide_reduce_fusion.11
  165.5 4.5 fusion.144
  169.9 6.1 divide_reduce_fusion.12
  176.9 4.5 fusion.142
  181.4 5.5 divide_reduce_fusion.10
  186.9 4.5 fusion.141
  191.4 5.6 divide_reduce_fusion.9
  197.8 1.7 copy.46
  201.4 31.9 %reduce-scatter.5.cloned.1.call-done = f32[2,16,1,256]{3,1,0,2:T(8,128)} async-done(((f32[2,16,8,256]{3,1,0,2:T(8,128)}), f32[2,16,1,256]{3,1,0,2:T(8,128)}) %reduce-scatter.5.cloned.1.call-update) | async-done | bytes 32784 | tf_op jit(solution)/shard_map/reduce_scatter | solution.py:59
  234.8 2.2 convolution_bitcast_fusion
  237.1 13.2 %psum.63 = bf16[2,1024]{1,0:T(2,128)(2,1)S(1)} all-reduce(f32[2,1024]{1,0:T(2,128)S(1)} %reshape.88), channel_id=1, replica_groups=mesh['cam'=8,'clip'=32] {'cam'}, use_global_device_ids=true, to_apply=%region_11.12 | all-reduce | flops 2048 | bytes 12288 | tf_op jit(solution)/shard_map/psum | solution.py:69
  251.7 43.0 %all-gather.1 = bf16[32,2,256]{2,1,0:T(2,128)(2,1)S(1)} all-gather(bf16[1,2,256]{2,1,0:T(2,128)(2,1)S(1)} %get-tuple-element.49), channel_id=1, replica_groups=mesh['cam'=8,'clip'=32] {'clip'}, dimensions={0}, use_global_device_ids=true | all-gather | bytes 33792 | tf_op jit(solution)/shard_map/all_gather | solution.py:75
  295.1 12.4 psum.64
  307.5 62.6 %psum.65 = f32[64]{0:T(128)S(1)} all-reduce(f32[64]{0:T(128)S(1)} %psum.64), channel_id=1, replica_groups=mesh['cam'=8,'clip'=32] {'clip'}, use_global_device_ids=true, to_apply=%region_17.18 | all-reduce | flops 64 | bytes 512 | tf_op jit(solution)/shard_map/psum | solution.py:88
  370.4 12.4 psum.66
  382.8 68.0 %psum.67 = f32[64]{0:T(128)S(1)} all-reduce(f32[64]{0:T(128)S(1)} %psum.66), channel_id=1, replica_groups=mesh['cam'=8,'clip'=32] {'clip'}, use_global_device_ids=true, to_apply=%region_21.22 | all-reduce | flops 64 | bytes 512 | tf_op jit(solution)/shard_map/psum | solution.py:88
  451.1 12.4 psum.68
  463.5 71.6 %psum.69 = f32[64]{0:T(128)S(1)} all-reduce(f32[64]{0:T(128)S(1)} %psum.68), channel_id=1, replica_groups=mesh['cam'=8,'clip'=32] {'clip'}, use_global_device_ids=true, to_apply=%region_25.26 | all-reduce | flops 64 | bytes 512 | tf_op jit(solution)/shard_map/psum | solution.py:88
  535.2 83.2 %psum.70 = f32[64]{0:T(128)S(1)} all-reduce(f32[64]{0:T(128)S(1)} %get-tuple-element.39), channel_id=1, replica_groups=mesh['cam'=8,'clip'=32] {'cam','clip'}, use_global_device_ids=true, to_apply=%region_27.28 | all-reduce | flops 64 | bytes 512 | tf_op jit(solution)/shard_map/psum | solution.py:83
  621.3 135.5 %all-reduce.3.cloned.1.call-done = f32[64,256]{1,0:T(8,128)} async-done(((f32[64,256]{1,0:T(8,128)}), f32[64,256]{1,0:T(8,128)}) %all-reduce.3.cloned.1.call-update) | async-done | bytes 65552
  757.4 12.4 psum.71
  771.3 2.7 fusion.52
  774.1 5.4 copy.35
  780.9 217.1 %reduce-scatter.9.cloned.1.call-done = f32[32,1024]{1,0:T(8,128)} async-done(((f32[1024,1024]{1,0:T(8,128)}), f32[32,1024]{1,0:T(8,128)}) %reduce-scatter.9.cloned.1.call-update) | async-done | bytes 131088 | tf_op jit(solution)/shard_map/reduce_scatter | solution.py:114
  999.1 218.5 %reduce-scatter.7.cloned.1.call-done = f32[32,256]{1,0:T(8,128)} async-done(((f32[1024,256]{1,0:T(8,128)}), f32[32,256]{1,0:T(8,128)}) %reduce-scatter.7.cloned.1.call-update) | async-done | bytes 32784 | tf_op jit(solution)/shard_map/reduce_scatter | solution.py:106
  1217.6 35.4 %reduce-scatter.11.cloned.1.call-done = f32[32,128]{1,0:T(8,128)} async-done(((f32[32,1024]{1,0:T(8,128)}), f32[32,128]{1,0:T(8,128)}) %reduce-scatter.11.cloned.1.call-update) | async-done | bytes 16400 | tf_op jit(solution)/shard_map/reduce_scatter | solution.py:122
  (75 shorter events, 22.7 us)
Async XLA Ops:
  7.2 1.6 copy-start
  7.2 9.2 copy-start.5
  7.2 60.4 %all-gather.4.cloned.1.call-start = ((), (), s32[]{:S(2)}) async-start(), calls=%async_computation.8 | async-start | bytes 9437184 | tf_op jit(solution)/shard_map/all_gather | solution.py:51
  12.3 221.0 %reduce-scatter.5.cloned.1.call-start = ((), (), s32[]{:S(2)}) async-start(), calls=%async_computation.4 | async-start | bytes 294912 | tf_op jit(solution)/shard_map/reduce_scatter | solution.py:59
  67.5 552.5 %copy-start.8 = (u32[256]{0:T(256)S(1)}, u32[256]{0:T(256)}, u32[]{:S(2)}) copy-start(u32[256]{0:T(256)} %constant.40) | copy-start | bytes 3076
  78.6 3.8 copy-start.3
  86.5 0.6 copy-start.2
  126.3 5.6 copy-start.6
  132.0 0.7 copy-start.7
  143.7 3.8 copy-start.3
  151.6 0.6 copy-start.2
  191.4 5.6 copy-start.6
  197.1 0.7 copy-start.7
  199.5 557.3 %all-reduce.3.cloned.1.call-start = ((), (), s32[]{:S(2)}) async-start(), calls=%async_computation.9 | async-start | bytes 131072
  620.0 378.1 %reduce-scatter.9.cloned.1.call-start = ((), (), s32[]{:S(2)}) async-start(), calls=%async_computation.6 | async-start | bytes 4325376 | tf_op jit(solution)/shard_map/reduce_scatter | solution.py:114
  771.3 481.6 %copy-start.1 = (bf16[1024,1024]{1,0:T(8,128)(2,1)S(1)}, bf16[1024,1024]{1,0:T(8,128)(2,1)}, u32[]{:S(2)}) copy-start(bf16[1024,1024]{1,0:T(8,128)(2,1)} %param.10) | copy-start | bytes 6291460
  774.1 224.0 %copy-start.4 = (bf16[256,256]{1,0:T(8,128)(2,1)S(1)}, bf16[256,256]{1,0:T(8,128)(2,1)}, u32[]{:S(2)}) copy-start(bf16[256,256]{1,0:T(8,128)(2,1)} %param.13) | copy-start | bytes 393220
  779.5 438.1 %reduce-scatter.7.cloned.1.call-start = ((), (), s32[]{:S(2)}) async-start(), calls=%async_computation.5 | async-start | bytes 1081344 | tf_op jit(solution)/shard_map/reduce_scatter | solution.py:106
  780.9 472.1 %reduce-scatter.11.cloned.1.call-start = ((), (), s32[]{:S(2)}) async-start(), calls=%async_computation.7 | async-start | bytes 147456 | tf_op jit(solution)/shard_map/reduce_scatter | solution.py:122
Sparse Core Ops, SparseCore 0:
  12.5 55.0 all-gather.3
  199.6 33.6 reduce-scatter.4
  620.1 136.6 all-reduce.2
  779.6 218.4 reduce-scatter.8
  1002.3 215.2 reduce-scatter.6
  1220.5 32.4 reduce-scatter.10
